TPU v7x, 128 devices: a whole 4x4x4 slice. The times are simulated.
128 devices in a mesh: row: 8 (over x, y_lo), col: 16 (over z, y_hi, core).
Axes of the slice: x: 4, y: 4 (y_hi: 2, y_lo: 2; y = y_hi * 2 + y_lo), z: 4, core: 2. Of those that a mesh axis runs over, the one named last changes fastest.
Arguments:
- amplitudes: float32 [16, 16, 256, 256], P('row', 'col'), may hold values from -6 to 6
- coulomb: bfloat16 [16, 16, 256, 256], P('row'), may hold values from -6 to 6
- inner_list: int32 [16, 16, 8], P('row', 'col'), may hold values from 0 to 15, as said below
- inner_count: int32 [16, 16], P('row', 'col'), may hold values from 4 to 8
- reader_list: int32 [16, 16, 8], P('row'), may hold values from 0 to 15, as said below
- reader_count: int32 [16, 16], P('row'), may hold values from 4 to 8
- virtual_energy: float32 [256], replicated, may hold values from 0.5 to 2.5
- occupied_energy: float32 [16], replicated, may hold values from -1.5 to -0.3
Outputs:
- new_amplitudes: float32 [16, 16, 256, 256], P('row', 'col')
Inputs may be any that keep to these rules, and one draw needn't show every extreme that they name: `inner_list`: for each pair block the 8 entries are distinct orbitals; only the first inner_count of them are used. `reader_list`: for each pair block the 8 entries are distinct orbitals; only the first reader_count of them are used.
All inputs are finite; a program needn't handle non-finite values.
Results may differ from a plain program's by a relative error of at most 0.0015.
Values may be sent and summed in bfloat16 or wider, within the bound.
A program may use at most 64 MiB of HBM per device.

v0:
```python
import jax
import jax.numpy as jnp
from jax import lax
from jax.sharding import PartitionSpec as P

ITERS = 2
damping = 0.5
coupling = 0.03125


def on_device(
    amplitudes,
    coulomb,
    inner_list,
    inner_count,
    reader_list,
    reader_count,
    virtual_energy,
    occupied_energy,
):
    orb_rows = amplitudes.shape[0]
    orb_cols = amplitudes.shape[1]
    slot_count = inner_list.shape[2]
    row_start = lax.axis_index("row") * orb_rows
    col_start = lax.axis_index("col") * orb_cols
    occ_rows = lax.dynamic_slice_in_dim(occupied_energy, row_start, orb_rows, 0)
    occ_cols = lax.dynamic_slice_in_dim(occupied_energy, col_start, orb_cols, 0)
    virt_pair = virtual_energy[:, None] + virtual_energy[None, :]
    denominator = (
        virt_pair[None, None] - occ_rows[:, None, None, None] - occ_cols[None, :, None, None]
    )
    slot_iota = jnp.arange(slot_count, dtype=jnp.int32)
    row_iota = jnp.arange(orb_rows, dtype=jnp.int32)[:, None, None]
    col_iota = jnp.arange(orb_cols, dtype=jnp.int32)[None, :, None]
    inner_mask = (slot_iota < inner_count[..., None]).astype(jnp.bfloat16)[..., None, None]
    own_readers = lax.dynamic_slice_in_dim(reader_list, col_start, orb_cols, 1)
    own_reader_len = lax.dynamic_slice_in_dim(reader_count, col_start, orb_cols, 1)
    reader_mask = (slot_iota < own_reader_len[..., None]).astype(jnp.bfloat16)[..., None, None]
    coulomb_own = lax.dynamic_slice_in_dim(coulomb, col_start, orb_cols, 1).astype(jnp.float32)
    left_inner = coulomb[row_iota, inner_list]
    amp_state = amplitudes
    for sweep_index in range(ITERS):
        amp_half = amp_state.astype(jnp.bfloat16)
        amp_columns = lax.all_gather(amp_half, "row", axis=0, tiled=True)
        right_inner = amp_columns[inner_list, col_iota] * inner_mask
        coupled = jnp.einsum(
            "ijsab,ijsbc->ijac", left_inner, right_inner, preferred_element_type=jnp.float32
        ).astype(jnp.bfloat16)
        coupled_columns = lax.all_gather(coupled, "row", axis=0, tiled=True)
        coupled_rows = lax.all_to_all(
            coupled_columns, "col", split_axis=0, concat_axis=1, tiled=True
        )
        mirror = jnp.transpose(
            lax.dynamic_slice_in_dim(coupled_rows, row_start, orb_rows, 1), (1, 0, 3, 2)
        )
        right_reader = coupled_columns[own_readers, col_iota] * reader_mask
        amp_rows = lax.all_gather(amp_half, "col", axis=1, tiled=True)
        left_reader = amp_rows[row_iota, own_readers]
        quadratic = jnp.einsum(
            "ijsab,ijsbc->ijac", left_reader, right_reader, preferred_element_type=jnp.float32
        )
        residual = (
            coulomb_own
            + coupling * (coupled.astype(jnp.float32) + mirror.astype(jnp.float32))
            + coupling * coupling * quadratic
        )
        amp_state = damping * amp_state - residual / denominator
    return amp_state


def solution(mesh):
    return jax.shard_map(
        on_device,
        mesh=mesh,
        in_specs=(
            P("row", "col", None, None),
            P("row", None, None, None),
            P("row", "col", None),
            P("row", "col"),
            P("row", None, None),
            P("row", None),
            P(),
            P(),
        ),
        out_specs=P("row", "col", None, None),
        check_vma=False,
    )
```

profile of v0, /device:TPU:1, one launch (start us, length us, event | category | flops | bytes accessed | tf_op | source)
XLA Modules:
  0.0 391.9 jit_solution(14267644027346781398)
XLA Ops:
  6.5 1.8 convert_element_type.66
  8.4 0.8 copy.51
  9.2 0.7 broadcast_compare_fusion
  9.9 0.7 broadcast_add_fusion.1
  10.7 0.1 select_reduce_fusion
  11.0 0.9 fusion.67
  12.1 2.9 gather_fusion
  15.0 46.9 %all-gather.9.cloned.1.call-done = bf16[16,1,256,256]{3,2,1,0:T(8,128)(2,1)} async-done(((bf16[2,1,256,256]{3,2,1,0:T(8,128)(2,1)}), bf16[16,1,256,256]{3,2,1,0:T(8,128)(2,1)}) %all-gather.9.cloned.1.call-update) | async-done | bytes 2097168 | tf_op jit(solution)/shard_map/all_gather | solution.py:44
  61.9 3.6 gather_fusion.1
  65.5 3.1 fusion.41
  68.7 0.7 all-gather.11.cloned.1.call-update
  69.4 51.3 %all-gather.17.cloned.1.call-done = bf16[16,256,256]{2,1,0:T(8,128)(2,1)} async-done(((bf16[2,256,256]{2,1,0:T(8,128)(2,1)}), bf16[16,256,256]{2,1,0:T(8,128)(2,1)}) %all-gather.17.cloned.1.call-update) | async-done | bytes 2097168 | tf_op jit(solution)/shard_map/all_gather | solution.py:49
  120.6 8.7 %all-to-all-start = ((bf16[16,1,256,256]{3,2,1,0:T(8,128)(2,1)}), bf16[16,1,256,256]{3,2,1,0:T(8,128)(2,1)}, u32[]{:S(2)}, u32[]{:S(2)}) async-start(bf16[16,1,256,256]{3,2,1,0:T(8,128)(2,1)} %bitcast.127), calls=%async_computation | async-start | bytes 4194304 | tf_op jit(solution)/shard_map/all_to_all | solution.py:50
  129.3 0.7 dynamic_slice.21
  130.1 0.2 fusion.68
  130.7 2.0 gather_fusion.3
  132.7 57.3 %all-gather.11.cloned.1.call-done = bf16[2,16,256,256]{3,2,1,0:T(8,128)(2,1)} async-done(((bf16[2,1,256,256]{3,2,1,0:T(8,128)(2,1)}), bf16[2,16,256,256]{3,2,1,0:T(8,128)(2,1)}) %all-gather.11.cloned.1.call-update) | async-done | bytes 4194320 | tf_op jit(solution)/shard_map/all_gather | solution.py:57
  190.1 4.2 %gather_fusion.2 = bf16[16,256,256]{2,1,0:T(8,128)(2,1)} fusion(bf16[2,16,256,256]{3,2,1,0:T(8,128)(2,1)} %all-gather.11.cloned.1.call-done, s32[16]{0:T(128)S(1)} %reshape.182), kind=kCustom, calls=%fused_computation.2 | custom fusion | bytes 4194432 | tf_op jit(solution)/shard_map/gather | solution.py:58
  194.3 1.0 constant_dynamic-slice_fusion.2
  195.3 0.9 copy.67
  196.1 4.2 %fusion.85 = (bf16[2,1,256,256]{3,2,0,1:T(8,128)(2,1)}, f32[2,1,256,256]{3,2,0,1:T(8,128)}) fusion(f32[]{:T(128)} %bitcast.20, f32[2]{0:T(128)S(1)} %dynamic_slice.20, f32[256,256]{1,0:T(8,128)S(1)} %broadcast_add_fusion, bf16[2,8,256,256]{3,2,1,0:T(8,128)(2,1)} %bitcast.136, bf16[2,8,256,256]{3,2,1,0:T(8,128)(2,1)S(1)} %bitcast.135, ...), kind=kOutput, calls=%fused_computation.88 | convolution fusion | flops 539754496 | bytes 6553648 | tf_op jit(solution)/shard_map/ijsab,ijsbc->ijac/dot_general | solution.py:59
  200.4 47.1 %all-gather.13.cloned.1.call-done = bf16[16,1,256,256]{3,2,1,0:T(8,128)(2,1)} async-done(((bf16[2,1,256,256]{3,2,1,0:T(8,128)(2,1)}), bf16[16,1,256,256]{3,2,1,0:T(8,128)(2,1)}) %all-gather.13.cloned.1.call-update) | async-done | bytes 2097168 | tf_op jit(solution)/shard_map/all_gather | solution.py:44
  247.4 3.6 gather_fusion.4
  251.1 3.1 fusion.38
  254.2 0.5 all-gather.15.cloned.1.call-update
  254.8 51.4 %all-gather.19.cloned.1.call-done = bf16[16,256,256]{2,1,0:T(8,128)(2,1)} async-done(((bf16[2,256,256]{2,1,0:T(8,128)(2,1)}), bf16[16,256,256]{2,1,0:T(8,128)(2,1)}) %all-gather.19.cloned.1.call-update) | async-done | bytes 2097168 | tf_op jit(solution)/shard_map/all_gather | solution.py:49
  306.2 8.7 %all-to-all-start.1 = ((bf16[16,1,256,256]{3,2,1,0:T(8,128)(2,1)}), bf16[16,1,256,256]{3,2,1,0:T(8,128)(2,1)}, u32[]{:S(2)}, u32[]{:S(2)}) async-start(bf16[16,1,256,256]{3,2,1,0:T(8,128)(2,1)} %bitcast.129), calls=%async_computation.1 | async-start | bytes 4194304 | tf_op jit(solution)/shard_map/all_to_all | solution.py:50
  314.9 2.0 gather_fusion.6
  316.9 58.7 %all-gather.15.cloned.1.call-done = bf16[2,16,256,256]{3,2,0,1:T(8,128)(2,1)} async-done(((bf16[2,1,256,256]{3,2,0,1:T(8,128)(2,1)}), bf16[2,16,256,256]{3,2,0,1:T(8,128)(2,1)}) %all-gather.15.cloned.1.call-update) | async-done | bytes 4194320 | tf_op jit(solution)/shard_map/all_gather | solution.py:57
  375.6 4.2 %gather_fusion.5 = bf16[16,256,256]{2,1,0:T(8,128)(2,1)} fusion(bf16[2,16,256,256]{3,2,0,1:T(8,128)(2,1)} %all-gather.15.cloned.1.call-done, s32[16]{0:T(128)S(1)} %reshape.182), kind=kCustom, calls=%fused_computation.5 | custom fusion | bytes 4194432 | tf_op jit(solution)/shard_map/gather | solution.py:58
  379.8 1.0 constant_dynamic-slice_fusion
  380.9 4.1 %fusion.52 = f32[2,1,256,256]{3,2,1,0:T(8,128)} fusion(bf16[2,8,256,256]{3,2,1,0:T(8,128)(2,1)} %bitcast.134, bf16[2,8,256,256]{3,2,1,0:T(8,128)(2,1)S(1)} %bitcast.133, bf16[2,8]{1,0:T(2,128)(2,1)S(1)} %compare_convert_fusion, f32[2,1,256,256]{3,2,0,1:T(8,128)} %get-tuple-element.8, bf16[2,1,256,256]{2,3,0,1:T(8,128)(2,1)S(1)} %copy.68, ...), kind=kOutput, calls=%fused_computation.31 | convolution fusion | flops 539623424 | bytes 6291504 | tf_op jit(solution)/shard_map/ijsab,ijsbc->ijac/dot_general | solution.py:59
  (58 shorter events, 1.4 us)
Async XLA Ops:
  6.5 123.5 %copy-start = (s32[2,16]{1,0:T(2,128)S(1)}, s32[2,16]{1,0:T(2,128)}, u32[]{:S(2)}) copy-start(s32[2,16]{1,0:T(2,128)} %param.13) | copy-start | bytes 388
  6.5 55.4 %all-gather.9.cloned.1.call-start = ((), (), s32[]{:S(2)}) async-start(), calls=%async_computation.2 | async-start | bytes 2359296 | tf_op jit(solution)/shard_map/all_gather | solution.py:44
  8.3 112.3 %all-gather.17.cloned.1.call-start = ((), (), s32[]{:S(2)}) async-start(), calls=%async_computation.6 | async-start | bytes 2359296 | tf_op jit(solution)/shard_map/all_gather | solution.py:49
  12.0 2.9 copy-start.11
  14.9 50.6 %copy-start.3 = (bf16[16,256,256]{2,1,0:T(8,128)(2,1)}, bf16[16,256,256]{2,1,0:T(8,128)(2,1)S(1)}, u32[]{:S(2)}) copy-start(bf16[16,256,256]{2,1,0:T(8,128)(2,1)S(1)} %gather_fusion) | copy-start | bytes 6291460
  68.6 121.4 %all-gather.11.cloned.1.call-start = ((), (), s32[]{:S(2)}) async-start(), calls=%async_computation.3 | async-start | bytes 4456448 | tf_op jit(solution)/shard_map/all_gather | solution.py:57
  120.6 8.7 %copy-start.12 = (f32[16]{0:T(128)S(1)}, f32[16]{0:T(128)}, u32[]{:S(2)}) copy-start(f32[16]{0:T(128)} %param.15) | copy-start | bytes 196
  120.6 9.9 %copy-start.10 = (f32[256]{0:T(256)S(1)}, f32[256]{0:T(256)}, u32[]{:S(2)}) copy-start(f32[256]{0:T(256)} %param.14) | copy-start | bytes 3076
  120.6 10.0 %copy-start.1 = (bf16[16,256,256]{2,1,0:T(8,128)(2,1)S(1)}, bf16[16,256,256]{2,1,0:T(8,128)(2,1)}, u32[]{:S(2)}) copy-start(bf16[16,256,256]{2,1,0:T(8,128)(2,1)} %all-gather.17.cloned.1.call-done) | copy-start | bytes 6291460
  120.6 73.7 %all-to-all-start = ((bf16[16,1,256,256]{3,2,1,0:T(8,128)(2,1)}), bf16[16,1,256,256]{3,2,1,0:T(8,128)(2,1)}, u32[]{:S(2)}, u32[]{:S(2)}) async-start(bf16[16,1,256,256]{3,2,1,0:T(8,128)(2,1)} %bitcast.127), calls=%async_computation | async-start | bytes 4194304 | tf_op jit(solution)/shard_map/all_to_all | solution.py:50
  129.3 118.2 %all-gather.13.cloned.1.call-start = ((), (), s32[]{:S(2)}) async-start(), calls=%async_computation.4 | async-start | bytes 2359296 | tf_op jit(solution)/shard_map/all_gather | solution.py:44
  132.7 63.4 %copy-start.6 = (bf16[16,256,256]{2,1,0:T(8,128)(2,1)S(1)}, bf16[16,256,256]{2,1,0:T(8,128)(2,1)}, u32[]{:S(2)}) copy-start(bf16[16,256,256]{2,1,0:T(8,128)(2,1)} %gather_fusion.3) | copy-start | bytes 6291460
  132.7 63.4 %copy-start.7 = (f32[2,1,256,256]{3,2,1,0:T(8,128)S(1)}, f32[2,1,256,256]{3,2,1,0:T(8,128)}, u32[]{:S(2)}) copy-start(f32[2,1,256,256]{3,2,1,0:T(8,128)} %param.8) | copy-start | bytes 1572868
  132.7 63.4 %copy-start.8 = (bf16[2,256,256]{2,1,0:T(8,128)(2,1)S(1)}, bf16[2,256,256]{2,1,0:T(8,128)(2,1)}, u32[]{:S(2)}) copy-start(bf16[2,256,256]{2,1,0:T(8,128)(2,1)} %fusion.41) | copy-start | bytes 786436
  200.3 50.7 %copy-start.4 = (bf16[16,256,256]{2,1,0:T(8,128)(2,1)S(1)}, bf16[16,256,256]{2,1,0:T(8,128)(2,1)}, u32[]{:S(2)}) copy-start(bf16[16,256,256]{2,1,0:T(8,128)(2,1)} %copy-done.3) | copy-start | bytes 6291460
  200.3 105.9 %all-gather.19.cloned.1.call-start = ((), (), s32[]{:S(2)}) async-start(), calls=%async_computation.7 | async-start | bytes 2359296 | tf_op jit(solution)/shard_map/all_gather | solution.py:49
  254.2 121.4 %all-gather.15.cloned.1.call-start = ((), (), s32[]{:S(2)}) async-start(), calls=%async_computation.5 | async-start | bytes 4456448 | tf_op jit(solution)/shard_map/all_gather | solution.py:57
  306.2 8.7 %copy-start.2 = (bf16[16,256,256]{2,1,0:T(8,128)(2,1)S(1)}, bf16[16,256,256]{2,1,0:T(8,128)(2,1)}, u32[]{:S(2)}) copy-start(bf16[16,256,256]{2,1,0:T(8,128)(2,1)} %all-gather.19.cloned.1.call-done) | copy-start | bytes 6291460
  306.2 73.6 %all-to-all-start.1 = ((bf16[16,1,256,256]{3,2,1,0:T(8,128)(2,1)}), bf16[16,1,256,256]{3,2,1,0:T(8,128)(2,1)}, u32[]{:S(2)}, u32[]{:S(2)}) async-start(bf16[16,1,256,256]{3,2,1,0:T(8,128)(2,1)} %bitcast.129), calls=%async_computation.1 | async-start | bytes 4194304 | tf_op jit(solution)/shard_map/all_to_all | solution.py:50
  316.9 64.1 %copy-start.5 = (bf16[16,256,256]{2,1,0:T(8,128)(2,1)S(1)}, bf16[16,256,256]{2,1,0:T(8,128)(2,1)}, u32[]{:S(2)}) copy-start(bf16[16,256,256]{2,1,0:T(8,128)(2,1)} %gather_fusion.6) | copy-start | bytes 6291460
  316.9 64.1 %copy-start.9 = (bf16[2,256,256]{2,1,0:T(8,128)(2,1)S(1)}, bf16[2,256,256]{2,1,0:T(8,128)(2,1)}, u32[]{:S(2)}) copy-start(bf16[2,256,256]{2,1,0:T(8,128)(2,1)} %fusion.38) | copy-start | bytes 786436
Sparse Core Ops, SparseCore 0:
  9.0 52.8 all-gather.8
  68.7 51.8 all-gather.16
  123.1 66.9 all-gather.10
  200.4 46.9 all-gather.12
  254.3 51.8 all-gather.18
  308.5 67.0 all-gather.14
where the time goes:
time: 393 us; the launch traced here: 392 us
  waiting for transfers between devices  314 us (80%)
  local copies, waits for them, and re-layouts  27.8 us (7%)
  starting transfers between devices  17.5 us (4%)
  matrix products  14.5 us (4%)
  between operations  13.6 us (3%)
  other arithmetic  4.55 us (1%)
    all_gather x2, waiting for transfers between devices, on_device(): amp_rows = lax.all_gather(amp_half, 'col', axis=1, tiled=True)  116 us
    all_gather x2, waiting for transfers between devices, on_device(): coupled_columns = lax.all_gather(coupled, 'row', axis=0, tiled=True)  103 us
    all_gather x2, waiting for transfers between devices, on_device(): amp_columns = lax.all_gather(amp_half, 'row', axis=0, tiled=True)  93.9 us
    all_to_all x2, starting transfers between devices, on_device(): lax.all_to_all(coupled_columns, 'col', split_axis=0, concat_axis=1, tiled...  17.3 us
    gather x2, local copies, waits for them, and re-layouts, on_device(): left_reader = amp_rows[row_iota, own_readers]  8.44 us
    dot_general x2, matrix products, on_device(): jnp.einsum('ijsab,ijsbc->ijac', left_reader, right_reader, preferred_elem...  8.3 us
  transfers between devices with their start and end apart: 8, of which 6 were waited for; matrix products, arithmetic and copies ran while one was open for 5% of the time, Pallas kernels for 0%

commit v1 on v0

--- a/solution.py
+++ b/solution.py
@@ -2,6 +2,7 @@
 import jax.numpy as jnp
 from jax import lax
 from jax.sharding import PartitionSpec as P
+from jax.lax import all_to_all, axis_size
 
 ITERS = 2
 damping = 0.5
@@ -54,7 +55,10 @@
             lax.dynamic_slice_in_dim(coupled_rows, row_start, orb_rows, 1), (1, 0, 3, 2)
         )
         right_reader = coupled_columns[own_readers, col_iota] * reader_mask
-        amp_rows = lax.all_gather(amp_half, "col", axis=1, tiled=True)
+        arr_now = axis_size("col")
+        f_now = jnp.stack(arr_now * [amp_half])
+        a_now = all_to_all(f_now, "col", 0, 0)
+        amp_rows = jnp.concatenate(a_now, axis=1)
         left_reader = amp_rows[row_iota, own_readers]
         quadratic = jnp.einsum(
             "ijsab,ijsbc->ijac", left_reader, right_reader, preferred_element_type=jnp.float32

time: 393 us -> 373 us (0.949)
  waiting for transfers between devices: 314 us -> 275 us
  starting transfers between devices: 17.5 us -> 32.6 us
    all_gather x2 -> x0, waiting for transfers between devices: 116 us -> none  [on_device(): amp_rows = lax.all_gather(amp_half, 'col', axis=1, tiled=True)]
    all_to_all x0 -> x2, waiting for transfers between devices: none -> 74.6 us  [on_device(): a_now = all_to_all(f_now, 'col', 0, 0)]
    all_gather x2, waiting for transfers between devices: 103 us -> 44.6 us  [on_device(): coupled_columns = lax.all_gather(coupled, 'row', axis=0, tiled=True)]
    all_to_all x2, waiting for transfers between devices: 0.01 us -> 42.7 us  [on_device(): lax.all_to_all(coupled_columns, 'col', split_axis=0, concat_axis=1, tiled...]
    all_gather x2, waiting for transfers between devices: 93.9 us -> 113 us  [on_device(): amp_columns = lax.all_gather(amp_half, 'row', axis=0, tiled=True)]
    all_to_all x0 -> x2, starting transfers between devices: none -> 14.9 us  [on_device(): a_now = all_to_all(f_now, 'col', 0, 0)]
    another operation x2 -> x4, local copies, waits for them, and re-layouts: 1.94 us -> 6.82 us  [the longest x2 4.89 us: on_device(): f_now = jnp.stack(arr_now * [amp_half])]
  transfers between devices with their start and end apart: 8 -> 8, of which waited for: 6 -> 8; matrix products, arithmetic and copies ran while one was open for 5% -> 10% of each run, Pallas kernels for 0% -> 0%
where the time goes in v1:
time: 373 us; the launch traced here: 372 us
  waiting for transfers between devices  275 us (74%)
  starting transfers between devices  32.6 us (9%)
  local copies, waits for them, and re-layouts  31.5 us (8%)
  matrix products  14.7 us (4%)
  between operations  13.3 us (4%)
  other arithmetic  4.31 us (1%)
    all_gather x2, waiting for transfers between devices, on_device(): amp_columns = lax.all_gather(amp_half, 'row', axis=0, tiled=True)  113 us
    all_to_all x2, waiting for transfers between devices, on_device(): a_now = all_to_all(f_now, 'col', 0, 0)  74.6 us
    all_gather x2, waiting for transfers between devices, on_device(): coupled_columns = lax.all_gather(coupled, 'row', axis=0, tiled=True)  44.6 us
    all_to_all x2, waiting for transfers between devices, on_device(): lax.all_to_all(coupled_columns, 'col', split_axis=0, concat_axis=1, tiled...  42.7 us
    all_to_all x2, starting transfers between devices, on_device(): lax.all_to_all(coupled_columns, 'col', split_axis=0, concat_axis=1, tiled...  17.6 us
    all_to_all x2, starting transfers between devices, on_device(): a_now = all_to_all(f_now, 'col', 0, 0)  14.9 us
    gather x2, local copies, waits for them, and re-layouts, on_device(): left_reader = amp_rows[row_iota, own_readers]  8.72 us
    dot_general x2, matrix products, on_device(): jnp.einsum('ijsab,ijsbc->ijac', left_reader, right_reader, preferred_elem...  8.5 us
  transfers between devices with their start and end apart: 8, of which 8 were waited for; matrix products, arithmetic and copies ran while one was open for 10% of the time, Pallas kernels for 0%

profile of v1, /device:TPU:1, one launch (start us, length us, event | category | flops | bytes accessed | tf_op | source)
XLA Modules:
  0.0 371.9 jit_solution(5672936811255771432)
XLA Ops:
  6.5 1.8 convert_element_type.70
  8.3 1.1 convert_bitcast_fusion.4
  9.4 2.4 stack.4
  11.9 9.6 %all-to-all-start.1 = ((bf16[16,2,1,256,256]{4,3,2,1,0:T(8,128)(2,1)}), bf16[16,2,1,256,256]{4,3,2,1,0:T(8,128)(2,1)}, u32[]{:S(2)}, u32[]{:S(2)}) async-start(bf16[16,2,1,256,256]{4,3,2,1,0:T(8,128)(2,1)} %stack.4), calls=%async_computation.1 | async-start | bytes 8388608 | tf_op jit(solution)/shard_map/all_to_all | solution.py:60
  21.8 0.2 fusion.67
  22.4 2.9 gather_fusion
  25.4 56.2 %all-gather.7.cloned.1.call-done = bf16[16,1,256,256]{3,2,1,0:T(8,128)(2,1)} async-done(((bf16[2,1,256,256]{3,2,1,0:T(8,128)(2,1)}), bf16[16,1,256,256]{3,2,1,0:T(8,128)(2,1)}) %all-gather.7.cloned.1.call-update) | async-done | bytes 2097168 | tf_op jit(solution)/shard_map/all_gather | solution.py:45
  81.6 3.6 gather_fusion.1
  85.2 3.1 fusion.41
  88.3 36.4 %all-to-all-done.1 = bf16[16,2,1,256,256]{4,3,2,1,0:T(8,128)(2,1)} async-done(((bf16[16,2,1,256,256]{4,3,2,1,0:T(8,128)(2,1)}), bf16[16,2,1,256,256]{4,3,2,1,0:T(8,128)(2,1)}, u32[]{:S(2)}, u32[]{:S(2)}) %all-to-all-start.1) | async-done | bytes 4194336 | tf_op jit(solution)/shard_map/all_to_all | solution.py:60
  124.6 22.6 %all-gather.11.cloned.1.call-done = bf16[16,256,256]{2,1,0:T(8,128)(2,1)} async-done(((bf16[2,256,256]{2,1,0:T(8,128)(2,1)}), bf16[16,256,256]{2,1,0:T(8,128)(2,1)}) %all-gather.11.cloned.1.call-update) | async-done | bytes 2097168 | tf_op jit(solution)/shard_map/all_gather | solution.py:50
  147.3 8.8 %all-to-all-start = ((bf16[16,1,256,256]{3,2,1,0:T(8,128)(2,1)}), bf16[16,1,256,256]{3,2,1,0:T(8,128)(2,1)}, u32[]{:S(2)}, u32[]{:S(2)}) async-start(bf16[16,1,256,256]{3,2,1,0:T(8,128)(2,1)} %bitcast.138), calls=%async_computation | async-start | bytes 4194304 | tf_op jit(solution)/shard_map/all_to_all | solution.py:51
  156.6 0.7 dynamic_slice.21
  157.5 4.4 %gather_fusion.2 = bf16[16,256,256]{2,1,0:T(8,128)(2,1)} fusion(bf16[2,16,256,256]{3,2,0,1:T(8,128)(2,1)} %bitcast.15, s32[16]{0:T(128)S(1)} %reshape.204), kind=kCustom, calls=%fused_computation.2 | custom fusion | bytes 4194432 | tf_op jit(solution)/shard_map/gather | solution.py:62
  161.9 2.0 gather_fusion.3
  163.9 20.7 %all-to-all-done = bf16[16,1,256,256]{3,2,1,0:T(8,128)(2,1)} async-done(((bf16[16,1,256,256]{3,2,1,0:T(8,128)(2,1)}), bf16[16,1,256,256]{3,2,1,0:T(8,128)(2,1)}, u32[]{:S(2)}, u32[]{:S(2)}) %all-to-all-start) | async-done | bytes 2097184 | tf_op jit(solution)/shard_map/all_to_all | solution.py:51
  184.5 1.0 constant_dynamic-slice_fusion.2
  185.7 3.9 %fusion.58 = f32[2,1,256,256]{3,2,0,1:T(8,128)S(1)} fusion(bf16[2,8,256,256]{3,2,1,0:T(8,128)(2,1)} %bitcast.146, bf16[2,8,256,256]{3,2,1,0:T(8,128)(2,1)} %bitcast.147, bf16[2,8]{1,0:T(2,128)(2,1)S(1)} %compare_convert_fusion, f32[2,1,256,256]{3,2,1,0:T(8,128)S(1)} %copy-done.3, bf16[2,1,256,256]{2,3,0,1:T(8,128)(2,1)S(1)} %copy.67, ...), kind=kOutput, calls=%fused_computation.33 | convolution fusion | flops 539623424 | bytes 6291504 | tf_op jit(solution)/shard_map/ijsab,ijsbc->ijac/dot_general | solution.py:63
  189.6 0.7 convert_bitcast_fusion.3
  190.3 2.4 stack.5
  192.8 5.3 %all-to-all-start.3 = ((bf16[16,2,1,256,256]{4,3,2,1,0:T(8,128)(2,1)}), bf16[16,2,1,256,256]{4,3,2,1,0:T(8,128)(2,1)}, u32[]{:S(2)}, u32[]{:S(2)}) async-start(bf16[16,2,1,256,256]{4,3,2,1,0:T(8,128)(2,1)} %stack.5), calls=%async_computation.3 | async-start | bytes 8388608 | tf_op jit(solution)/shard_map/all_to_all | solution.py:60
  198.1 57.3 %all-gather.9.cloned.1.call-done = bf16[16,1,256,256]{3,2,1,0:T(8,128)(2,1)} async-done(((bf16[2,1,256,256]{3,2,1,0:T(8,128)(2,1)}), bf16[16,1,256,256]{3,2,1,0:T(8,128)(2,1)}) %all-gather.9.cloned.1.call-update) | async-done | bytes 2097168 | tf_op jit(solution)/shard_map/all_gather | solution.py:45
  255.4 3.6 gather_fusion.4
  259.0 3.1 fusion.38
  262.1 38.3 %all-to-all-done.3 = bf16[16,2,1,256,256]{4,3,2,1,0:T(8,128)(2,1)} async-done(((bf16[16,2,1,256,256]{4,3,2,1,0:T(8,128)(2,1)}), bf16[16,2,1,256,256]{4,3,2,1,0:T(8,128)(2,1)}, u32[]{:S(2)}, u32[]{:S(2)}) %all-to-all-start.3) | async-done | bytes 4194336 | tf_op jit(solution)/shard_map/all_to_all | solution.py:60
  300.4 21.9 %all-gather.13.cloned.1.call-done = bf16[16,256,256]{2,1,0:T(8,128)(2,1)} async-done(((bf16[2,256,256]{2,1,0:T(8,128)(2,1)}), bf16[16,256,256]{2,1,0:T(8,128)(2,1)}) %all-gather.13.cloned.1.call-update) | async-done | bytes 2097168 | tf_op jit(solution)/shard_map/all_gather | solution.py:50
  322.3 8.8 %all-to-all-start.2 = ((bf16[16,1,256,256]{3,2,1,0:T(8,128)(2,1)}), bf16[16,1,256,256]{3,2,1,0:T(8,128)(2,1)}, u32[]{:S(2)}, u32[]{:S(2)}) async-start(bf16[16,1,256,256]{3,2,1,0:T(8,128)(2,1)} %bitcast.140), calls=%async_computation.2 | async-start | bytes 4194304 | tf_op jit(solution)/shard_map/all_to_all | solution.py:51
  331.2 4.4 %gather_fusion.5 = bf16[16,256,256]{2,1,0:T(8,128)(2,1)} fusion(bf16[2,16,256,256]{3,2,0,1:T(8,128)(2,1)} %bitcast.35, s32[16]{0:T(128)S(1)} %reshape.204), kind=kCustom, calls=%fused_computation.5 | custom fusion | bytes 4194432 | tf_op jit(solution)/shard_map/gather | solution.py:62
  335.5 2.0 gather_fusion.6
  337.6 22.1 %all-to-all-done.2 = bf16[16,1,256,256]{3,2,1,0:T(8,128)(2,1)} async-done(((bf16[16,1,256,256]{3,2,1,0:T(8,128)(2,1)}), bf16[16,1,256,256]{3,2,1,0:T(8,128)(2,1)}, u32[]{:S(2)}, u32[]{:S(2)}) %all-to-all-start.2) | async-done | bytes 2097184 | tf_op jit(solution)/shard_map/all_to_all | solution.py:51
  359.6 1.0 constant_dynamic-slice_fusion
  360.7 4.6 %fusion.52 = f32[2,1,256,256]{3,2,1,0:T(8,128)} fusion(bf16[2,8,256,256]{3,2,1,0:T(8,128)(2,1)} %bitcast.144, bf16[2,8,256,256]{3,2,1,0:T(8,128)(2,1)} %bitcast.145, bf16[2,8]{1,0:T(2,128)(2,1)S(1)} %compare_convert_fusion, f32[2,1,256,256]{3,2,0,1:T(8,128)S(1)} %fusion.58, bf16[2,1,256,256]{2,3,0,1:T(8,128)(2,1)S(1)} %copy.68, ...), kind=kOutput, calls=%fused_computation.31 | convolution fusion | flops 539623424 | bytes 6291504 | tf_op jit(solution)/shard_map/ijsab,ijsbc->ijac/dot_general | solution.py:63
  (58 shorter events, 1.9 us)
Async XLA Ops:
  6.5 149.8 %copy-start = (s32[2,16]{1,0:T(2,128)S(1)}, s32[2,16]{1,0:T(2,128)}, u32[]{:S(2)}) copy-start(s32[2,16]{1,0:T(2,128)} %param.13) | copy-start | bytes 388
  6.5 75.0 %all-gather.7.cloned.1.call-start = ((), (), s32[]{:S(2)}) async-start(), calls=%async_computation.4 | async-start | bytes 2359296 | tf_op jit(solution)/shard_map/all_gather | solution.py:45
  11.9 9.6 %copy-start.7 = (s32[2,1,8]{2,1,0:T(1,128)S(1)}, s32[2,1,8]{2,1,0:T(1,128)}, u32[]{:S(2)}) copy-start(s32[2,1,8]{2,1,0:T(1,128)} %param.10) | copy-start | bytes 196
  11.9 9.9 %copy-start.8 = (s32[2,16,8]{1,2,0:T(8,128)S(1)}, s32[2,16,8]{1,2,0:T(8,128)}, u32[]{:S(2)}) copy-start(s32[2,16,8]{1,2,0:T(8,128)} %param.12) | copy-start | bytes 3076
  11.9 112.8 %all-to-all-start.1 = ((bf16[16,2,1,256,256]{4,3,2,1,0:T(8,128)(2,1)}), bf16[16,2,1,256,256]{4,3,2,1,0:T(8,128)(2,1)}, u32[]{:S(2)}, u32[]{:S(2)}) async-start(bf16[16,2,1,256,256]{4,3,2,1,0:T(8,128)(2,1)} %stack.4), calls=%async_computation.1 | async-start | bytes 8388608 | tf_op jit(solution)/shard_map/all_to_all | solution.py:60
  21.4 125.8 %all-gather.11.cloned.1.call-start = ((), (), s32[]{:S(2)}) async-start(), calls=%async_computation.6 | async-start | bytes 2359296 | tf_op jit(solution)/shard_map/all_gather | solution.py:50
  22.4 2.9 copy-start.10
  25.3 59.9 %copy-start.4 = (bf16[16,256,256]{2,1,0:T(8,128)(2,1)}, bf16[16,256,256]{2,1,0:T(8,128)(2,1)S(1)}, u32[]{:S(2)}) copy-start(bf16[16,256,256]{2,1,0:T(8,128)(2,1)S(1)} %gather_fusion) | copy-start | bytes 6291460
  147.3 9.3 %copy-start.11 = (f32[16]{0:T(128)S(1)}, f32[16]{0:T(128)}, u32[]{:S(2)}) copy-start(f32[16]{0:T(128)} %param.15) | copy-start | bytes 196
  147.3 10.1 %copy-start.9 = (f32[256]{0:T(256)S(1)}, f32[256]{0:T(256)}, u32[]{:S(2)}) copy-start(f32[256]{0:T(256)} %param.14) | copy-start | bytes 3076
  147.3 37.2 %all-to-all-start = ((bf16[16,1,256,256]{3,2,1,0:T(8,128)(2,1)}), bf16[16,1,256,256]{3,2,1,0:T(8,128)(2,1)}, u32[]{:S(2)}, u32[]{:S(2)}) async-start(bf16[16,1,256,256]{3,2,1,0:T(8,128)(2,1)} %bitcast.138), calls=%async_computation | async-start | bytes 4194304 | tf_op jit(solution)/shard_map/all_to_all | solution.py:51
  156.1 99.3 %all-gather.9.cloned.1.call-start = ((), (), s32[]{:S(2)}) async-start(), calls=%async_computation.5 | async-start | bytes 2359296 | tf_op jit(solution)/shard_map/all_gather | solution.py:45
  157.5 4.4 %copy-start.1 = (bf16[16,256,256]{2,1,0:T(8,128)(2,1)S(1)}, bf16[16,256,256]{2,1,0:T(8,128)(2,1)}, u32[]{:S(2)}) copy-start(bf16[16,256,256]{2,1,0:T(8,128)(2,1)} %all-gather.11.cloned.1.call-done) | copy-start | bytes 6291460
  161.9 23.8 %copy-start.3 = (f32[2,1,256,256]{3,2,1,0:T(8,128)S(1)}, f32[2,1,256,256]{3,2,1,0:T(8,128)}, u32[]{:S(2)}) copy-start(f32[2,1,256,256]{3,2,1,0:T(8,128)} %param.8) | copy-start | bytes 1572868
  192.8 107.6 %all-to-all-start.3 = ((bf16[16,2,1,256,256]{4,3,2,1,0:T(8,128)(2,1)}), bf16[16,2,1,256,256]{4,3,2,1,0:T(8,128)(2,1)}, u32[]{:S(2)}, u32[]{:S(2)}) async-start(bf16[16,2,1,256,256]{4,3,2,1,0:T(8,128)(2,1)} %stack.5), calls=%async_computation.3 | async-start | bytes 8388608 | tf_op jit(solution)/shard_map/all_to_all | solution.py:60
  198.1 60.9 %copy-start.5 = (bf16[16,256,256]{2,1,0:T(8,128)(2,1)S(1)}, bf16[16,256,256]{2,1,0:T(8,128)(2,1)}, u32[]{:S(2)}) copy-start(bf16[16,256,256]{2,1,0:T(8,128)(2,1)} %copy-done.4) | copy-start | bytes 6291460
  198.1 124.3 %all-gather.13.cloned.1.call-start = ((), (), s32[]{:S(2)}) async-start(), calls=%async_computation.7 | async-start | bytes 2359296 | tf_op jit(solution)/shard_map/all_gather | solution.py:50
  322.3 37.3 %all-to-all-start.2 = ((bf16[16,1,256,256]{3,2,1,0:T(8,128)(2,1)}), bf16[16,1,256,256]{3,2,1,0:T(8,128)(2,1)}, u32[]{:S(2)}, u32[]{:S(2)}) async-start(bf16[16,1,256,256]{3,2,1,0:T(8,128)(2,1)} %bitcast.140), calls=%async_computation.2 | async-start | bytes 4194304 | tf_op jit(solution)/shard_map/all_to_all | solution.py:51
  331.2 4.4 %copy-start.2 = (bf16[16,256,256]{2,1,0:T(8,128)(2,1)S(1)}, bf16[16,256,256]{2,1,0:T(8,128)(2,1)}, u32[]{:S(2)}) copy-start(bf16[16,256,256]{2,1,0:T(8,128)(2,1)} %all-gather.13.cloned.1.call-done) | copy-start | bytes 6291460
  335.5 25.2 %copy-start.6 = (bf16[2,256,256]{2,1,0:T(8,128)(2,1)S(1)}, bf16[2,256,256]{2,1,0:T(8,128)(2,1)}, u32[]{:S(2)}) copy-start(bf16[2,256,256]{2,1,0:T(8,128)(2,1)} %fusion.38) | copy-start | bytes 786436
Sparse Core Ops, SparseCore 0:
  9.0 72.5 all-gather.6
  88.4 58.8 all-gather.10
  190.5 64.8 all-gather.8
  262.2 60.0 all-gather.12
